TPU v7x, 256 devices: a whole 4x4x8 slice. The times are simulated.
256 devices in a mesh: seq: 64 (over z, x, core), head: 4 (over y).
Axes of the slice: x: 4, y: 4, z: 8, core: 2. Of those that a mesh axis runs over, the one named last changes fastest.
Arguments:
- queries: bfloat16 [32768, 4096], P(('seq', 'head')), may hold values from -6 to 6
- keys: bfloat16 [32768, 4096], P(('seq', 'head')), may hold values from -6 to 6
- values: bfloat16 [32768, 4096], P(('seq', 'head')), may hold values from -128 to 128
- out_grad: bfloat16 [32768, 4096], P(('seq', 'head')), may hold values from -16 to 16
- doc_lengths: int32 [8], replicated, may hold values from 1 to 16384, 32768 in all
Outputs:
- attn_out: bfloat16 [32768, 4096], P(('seq', 'head'))
- grad_queries: bfloat16 [32768, 4096], P(('seq', 'head'))
- grad_keys: bfloat16 [32768, 4096], P(('seq', 'head'))
- grad_values: bfloat16 [32768, 4096], P(('seq', 'head'))
Inputs may be any that keep to these rules, and one draw needn't show every extreme that they name: `doc_lengths`: the lengths sum to 32768; the longest is exactly 16384.
All inputs are finite; a program needn't handle non-finite values.
Results may differ from a plain program's by a relative error of at most 0.011.
Values may be sent and summed in bfloat16 or wider, within the bound.
A program may use at most 128 MiB of HBM per device.

v0:
```python
import jax
import jax.numpy as jnp
from jax import lax
from jax.sharding import PartitionSpec as P

DH = 128


def prefix(value, axis, join, neutral):
    count, mine = (lax.axis_size(axis), lax.axis_index(axis))
    pieces = jax.tree.map(lambda part: lax.all_gather(part, axis), value)
    so_far = jax.tree.map(
        lambda part, zero: jnp.full_like(part, 0) + jnp.asarray(zero, part.dtype), value, neutral
    )

    def lap(position, so_far):
        longer = join(so_far, jax.tree.map(lambda part: part[position], pieces))
        return jax.tree.map(lambda new, old: jnp.where(position < mine, new, old), longer, so_far)

    return lax.fori_loop(0, count - 1, lap, so_far)


def prefix_2(array, axis, join, neutral):
    count = lax.axis_size(axis)
    place = lax.axis_index(axis)
    ahead = count - 1 - place
    gathered = jax.tree.map(
        lambda a, kind: lax.all_gather(a.astype(kind), axis), array, (jnp.bfloat16, jnp.bfloat16)
    )
    state = jax.tree.map(lambda a, e: jnp.zeros_like(a) + jnp.asarray(e, a.dtype), array, neutral)

    def one(lap, state):
        source = count - 1 - lap
        return join(
            state,
            jax.tree.map(
                lambda a, own: lax.dynamic_index_in_dim(a, source, 0, False).astype(own.dtype),
                gathered,
                array,
            ),
        )

    return lax.fori_loop(0, ahead, one, state)


def feature(array):
    wide = array.astype(jnp.float32)
    return jnp.where(wide > 0, wide + 1.0, jnp.exp(jnp.minimum(wide, 0.0)))


def slope(array):
    wide = array.astype(jnp.float32)
    return jnp.where(wide > 0, 1.0, jnp.exp(jnp.minimum(wide, 0.0)))


def doc_index(doc_ends, where):
    return jnp.sum((jnp.asarray(where)[..., None] >= doc_ends).astype(jnp.int32), axis=-1)


def linked(earlier, later):
    return (later[0] + (1.0 - later[1]) * earlier[0], jnp.maximum(earlier[1], later[1]))


def local(queries, keys, values, out_grad, doc_lengths):
    shared = (
        lax.all_to_all(queries, "head", split_axis=1, concat_axis=0, tiled=True),
        lax.all_to_all(keys, "head", split_axis=1, concat_axis=0, tiled=True),
        lax.all_to_all(values, "head", split_axis=1, concat_axis=0, tiled=True),
        lax.all_to_all(out_grad, "head", split_axis=1, concat_axis=0, tiled=True),
    )
    block_len = shared[0].shape[0]
    head_count = shared[0].shape[1] // DH
    query_rows = shared[0].reshape(block_len, head_count, DH)
    key_rows = shared[1].reshape(block_len, head_count, DH)
    value_rows = shared[2].reshape(block_len, head_count, DH)
    grad_rows = shared[3].reshape(block_len, head_count, DH)
    block_index = lax.axis_index("seq")
    doc_ends = jnp.cumsum(doc_lengths)
    block_start = block_index * block_len
    within = jnp.arange(block_len, dtype=jnp.int32)
    doc_of = doc_index(doc_ends, block_start + within)
    doc_first = doc_of[0]
    doc_last = doc_of[block_len - 1]
    before = doc_index(doc_ends, block_start - 1)
    doc_after = doc_index(doc_ends, block_start + block_len)
    visible = (within[:, None] >= within[None, :]) & (doc_of[:, None] == doc_of[None, :])
    head_rows = (doc_of == doc_first)[:, None, None]
    tail_rows = (doc_of == doc_last)[:, None, None]
    tile_rows = 256
    tile_count = block_len // tile_rows
    feat_query = feature(query_rows).astype(jnp.bfloat16)
    feat_key = feature(key_rows).astype(jnp.bfloat16)
    zero_bf = jnp.zeros((), jnp.bfloat16)
    tail_state = jnp.einsum(
        "shd,she->hde",
        jnp.where(tail_rows, feat_key, zero_bf),
        value_rows,
        preferred_element_type=jnp.float32,
    )
    reset_flag = (doc_last != before).astype(jnp.float32)
    carried, _ = prefix(
        (tail_state, reset_flag),
        "seq",
        linked,
        (jnp.zeros_like(tail_state), jnp.zeros((), jnp.float32)),
    )
    incoming = jnp.where(doc_first == before, carried, 0.0).astype(jnp.bfloat16)
    score_tiles = []
    normed_tiles = []
    grad_att_tiles = []
    for tile in range(tile_count):
        first = tile * tile_rows
        last = first + tile_rows
        query_tile = feat_query[first:last]
        tile_scores = jnp.einsum(
            "thd,shd->hts", query_tile, feat_key[:last], preferred_element_type=jnp.float32
        )
        tile_scores = jnp.where(visible[first:last, :last][None], tile_scores, 0.0).astype(
            jnp.bfloat16
        )
        attended = jnp.einsum(
            "hts,she->the", tile_scores, value_rows[:last], preferred_element_type=jnp.float32
        )
        attended = attended + jnp.where(
            head_rows[first:last],
            jnp.einsum("thd,hde->the", query_tile, incoming, preferred_element_type=jnp.float32),
            0.0,
        )
        inv_rms = lax.rsqrt(jnp.mean(attended * attended, axis=-1, keepdims=True) + 1e-05)
        normed = attended * inv_rms
        grad_out = grad_rows[first:last].astype(jnp.float32)
        grad_att_tile = (
            (grad_out - normed * jnp.mean(grad_out * normed, axis=-1, keepdims=True)) * inv_rms
        ).astype(jnp.bfloat16)
        score_tiles.append(tile_scores)
        normed_tiles.append(normed.astype(jnp.bfloat16))
        grad_att_tiles.append(grad_att_tile)
    out_block = jnp.concatenate(normed_tiles, axis=0).reshape(block_len, head_count * DH)
    grad_att = jnp.concatenate(grad_att_tiles, axis=0)
    attn_out = lax.all_to_all(out_block, "head", split_axis=0, concat_axis=1, tiled=True)
    head_sum = jnp.einsum(
        "thd,the->hde",
        jnp.where(head_rows, feat_query, zero_bf),
        grad_att,
        preferred_element_type=jnp.float32,
    )
    reset_back = (doc_first != doc_after).astype(jnp.float32)
    future, _ = prefix_2(
        (head_sum, reset_back),
        "seq",
        linked,
        (jnp.zeros_like(head_sum), jnp.zeros((), jnp.float32)),
    )
    outgoing = jnp.where(doc_last == doc_after, future, 0.0).astype(jnp.bfloat16)
    grad_fk = jnp.zeros((block_len, head_count, DH), jnp.float32)
    grad_fv = jnp.zeros((block_len, head_count, DH), jnp.float32)
    grad_fq_tiles = []
    for tile in range(tile_count):
        first = tile * tile_rows
        last = first + tile_rows
        grad_tile = grad_att_tiles[tile]
        tile_grads = jnp.einsum(
            "the,she->hts", grad_tile, value_rows[:last], preferred_element_type=jnp.float32
        )
        tile_grads = jnp.where(visible[first:last, :last][None], tile_grads, 0.0).astype(
            jnp.bfloat16
        )
        grad_fq_tile = jnp.einsum(
            "hts,shd->thd", tile_grads, feat_key[:last], preferred_element_type=jnp.float32
        )
        grad_fq_tile = grad_fq_tile + jnp.where(
            head_rows[first:last],
            jnp.einsum("the,hde->thd", grad_tile, incoming, preferred_element_type=jnp.float32),
            0.0,
        )
        grad_fq_tiles.append(grad_fq_tile)
        grad_fk = grad_fk.at[:last].add(
            jnp.einsum(
                "hts,thd->shd",
                tile_grads,
                feat_query[first:last],
                preferred_element_type=jnp.float32,
            )
        )
        grad_fv = grad_fv.at[:last].add(
            jnp.einsum(
                "hts,the->she", score_tiles[tile], grad_tile, preferred_element_type=jnp.float32
            )
        )
    grad_fq = jnp.concatenate(grad_fq_tiles, axis=0)
    grad_fk = grad_fk + jnp.where(
        tail_rows,
        jnp.einsum("she,hde->shd", value_rows, outgoing, preferred_element_type=jnp.float32),
        0.0,
    )
    grad_fv = grad_fv + jnp.where(
        tail_rows,
        jnp.einsum("shd,hde->she", feat_key, outgoing, preferred_element_type=jnp.float32),
        0.0,
    )
    grad_query = (
        (grad_fq * slope(query_rows)).astype(jnp.bfloat16).reshape(block_len, head_count * DH)
    )
    grad_key = (grad_fk * slope(key_rows)).astype(jnp.bfloat16).reshape(block_len, head_count * DH)
    grad_value = grad_fv.astype(jnp.bfloat16).reshape(block_len, head_count * DH)
    grad_queries, grad_keys, grad_values = (
        lax.all_to_all(grad_query, "head", split_axis=0, concat_axis=1, tiled=True),
        lax.all_to_all(grad_key, "head", split_axis=0, concat_axis=1, tiled=True),
        lax.all_to_all(grad_value, "head", split_axis=0, concat_axis=1, tiled=True),
    )
    return (attn_out, grad_queries, grad_keys, grad_values)


def solution(mesh):
    placed = (
        P(("seq", "head"), None),
        P(("seq", "head"), None),
        P(("seq", "head"), None),
        P(("seq", "head"), None),
        P(),
    )
    return jax.shard_map(
        local,
        mesh=mesh,
        in_specs=placed,
        out_specs=(
            P(("seq", "head"), None),
            P(("seq", "head"), None),
            P(("seq", "head"), None),
            P(("seq", "head"), None),
        ),
        check_vma=False,
    )
```

profile of v0, /device:TPU:8, one launch (start us, length us, event | category | flops | bytes accessed | tf_op | source)
XLA Modules:
  0.0 783.8 jit_solution(12176665650693809135)
XLA Ops:
  7.2 2.4 copy.285
  9.5 5.8 all-to-all-start.1
  16.6 11.7 %all-to-all-done.1 = bf16[128,4,1024]{2,0,1:T(8,128)(2,1)S(1)} async-done(((bf16[128,4,1024]{2,0,1:T(8,128)(2,1)}), bf16[128,4,1024]{2,0,1:T(8,128)(2,1)S(1)}, u32[]{:S(2)}, u32[]{:S(2)}) %all-to-all-start.1) | async-done | bytes 1048608 | tf_op jit(solution)/shard_map/all_to_all | solution.py:67
  28.2 4.9 all-to-all-start.2
  37.7 7.5 all-to-all-done.2
  49.8 5.8 all-to-all-start
  59.1 2.3 copy.283
  62.7 134.0 %all-reduce.2 = f32[64]{0:T(128)S(1)} all-reduce(f32[64]{0:T(128)S(1)} %dynamic-update-slice.10), channel_id=1, replica_groups=mesh['seq'=64,'head'=4] {'seq'}, use_global_device_ids=true, to_apply=%add.2 | all-reduce | flops 64 | bytes 512
  196.8 4.7 all-to-all-start.4
  201.5 2.7 fusion.2
  213.7 2.5 slice_convert_fusion.1
  220.3 2.5 copy.250
  223.1 2.8 bitcast_select_fusion
  232.7 168.2 %while.35 = (s32[]{:T(128)}, f32[8,128,128]{2,1,0:T(8,128)S(1)}, s32[]{:T(128)}, f32[64,8,128,128]{3,2,1,0:T(8,128)}, f32[64]{0:T(128)S(1)}, /*index=5*/s32[]{:T(128)}, f32[1]{0:T(128)}, s32[]{:T(128)}) while((s32[]{:T(128)}, f32[8,128,128]{2,1,0:T(8,128)S(1)}, s32[]{:T(128)}, f32[64,8,128,128]{3,2,1,0:T(8,128)}, f32[64]{0:T(128)S(1)}, ...), condition=%wide.region_4.5_spmd.clone, body=%wide.region_3.4_spmd.clone.sunk | while | flops 524293 | bytes 1573001 | solution.py:20
  412.2 2.5 copy.201
  418.2 2.6 copy.208
  420.8 2.9 pad_maximum_fusion
  423.7 2.9 copy.236
  426.6 3.4 fusion.7
  430.0 5.4 all-to-all-start.5
  438.7 126.2 %all-reduce.3 = bf16[64]{0:T(256)(128)(2,1)S(1)} all-reduce(bf16[64]{0:T(256)(128)(2,1)S(1)} %dynamic-update-slice.11), channel_id=1, replica_groups=mesh['seq'=64,'head'=4] {'seq'}, use_global_device_ids=true, to_apply=%add.3 | all-reduce | flops 64 | bytes 256
  564.9 3.4 copy.252
  568.3 3.0 copy.237
  573.0 2.3 all_to_all.105
  575.4 2.5 convolution_bitcast_fusion.1
  579.8 4.8 all-to-all-start.3
  584.6 153.4 %while.34 = (s32[]{:T(128)}, f32[8,128,128]{2,1,0:T(8,128)S(1)}, s32[]{:T(128)}, bf16[64,8,128,128]{3,2,1,0:T(8,128)(2,1)}, bf16[64]{0:T(256)(128)(2,1)S(1)}, /*...) while((s32[]{:T(128)}, f32[8,128,128]{2,1,0:T(8,128)S(1)}, s32[]{:T(128)}, ...), condition=%wide.region_11.12_spmd, body=%wide.region_10.11_spmd.sunk | while | flops 393223 | bytes 1310893 | solution.py:43
  738.0 3.4 fusion.12
  743.5 2.4 copy.221
  745.9 4.9 all-to-all-start.7
  756.4 4.9 all-to-all-done.7
  761.2 4.9 all-to-all-start.6
  (404 shorter events, 311.2 us)
Async XLA Ops:
  7.2 8.2 %copy-start.29 = (bf16[128,4096]{1,0:T(8,128)(2,1)S(1)}, bf16[128,4096]{1,0:T(8,128)(2,1)}, u32[]{:S(2)}) copy-start(bf16[128,4096]{1,0:T(8,128)(2,1)} %param.23) | copy-start | bytes 3145732
  9.5 6.8 copy-start.33
  9.5 18.7 %all-to-all-start.1 = ((bf16[128,4,1024]{2,0,1:T(8,128)(2,1)}), bf16[128,4,1024]{2,0,1:T(8,128)(2,1)S(1)}, u32[]{:S(2)}, u32[]{:S(2)}) async-start(bf16[128,4,1024]{2,0,1:T(8,128)(2,1)} %bitcast.161), calls=%async_computation.1 | async-start | bytes 2097152 | tf_op jit(solution)/shard_map/all_to_all | solution.py:67
  28.2 17.0 %all-to-all-start.2 = ((bf16[128,4,1024]{2,0,1:T(8,128)(2,1)}), bf16[128,4,1024]{2,0,1:T(8,128)(2,1)S(1)}, u32[]{:S(2)}, u32[]{:S(2)}) async-start(bf16[128,4,1024]{2,0,1:T(8,128)(2,1)} %bitcast.160), calls=%async_computation.2 | async-start | bytes 2097152 | tf_op jit(solution)/shard_map/all_to_all | solution.py:68
  33.2 199.6 %all-gather.5.cloned.1.call-start = ((), (), s32[]{:S(2)}) async-start(), calls=%async_computation.8 | async-start | bytes 34078720 | tf_op jit(solution)/shard_map/all_gather | solution.py:11
  49.8 11.7 %copy-start.34 = (u32[256]{0:T(256)S(1)}, u32[256]{0:T(256)}, u32[]{:S(2)}) copy-start(u32[256]{0:T(256)} %constant.223) | copy-start | bytes 3076
  49.8 146.9 %all-to-all-start = ((bf16[128,4,1024]{2,0,1:T(8,128)(2,1)}), bf16[128,4,1024]{2,0,1:T(8,128)(2,1)}, u32[]{:S(2)}, u32[]{:S(2)}) async-start(bf16[128,4,1024]{2,0,1:T(8,128)(2,1)} %bitcast.162), calls=%async_computation | async-start | bytes 2097152 | tf_op jit(solution)/shard_map/all_to_all | solution.py:66
  59.1 169.7 %copy-start.31 = (pred[256,512]{1,0:T(8,128)(4,1)}, pred[256,512]{1,0:T(8,128)(4,1)S(1)}, u32[]{:S(2)}) copy-start(pred[256,512]{1,0:T(8,128)(4,1)S(1)} %slice.160) | copy-start | bytes 393220
  196.8 16.9 %all-to-all-start.4 = ((bf16[128,4,1024]{2,0,1:T(8,128)(2,1)}), bf16[128,4,1024]{2,0,1:T(8,128)(2,1)}, u32[]{:S(2)}, u32[]{:S(2)}) async-start(bf16[128,4,1024]{2,0,1:T(8,128)(2,1)} %bitcast.191), calls=%async_computation.4 | async-start | bytes 2097152 | tf_op jit(solution)/shard_map/all_to_all | solution.py:69
  201.5 383.1 %all-gather.7.cloned.1.call-start = ((), (), s32[]{:S(2)}) async-start(), calls=%async_computation.9 | async-start | bytes 17039360 | tf_op jit(solution)/shard_map/all_gather | solution.py:28
  207.3 193.7 %copy-start.4 = (bf16[256,8,128]{0,2,1:T(8,128)(2,1)}, bf16[256,8,128]{0,2,1:T(8,128)(2,1)S(1)}, u32[]{:S(2)}) copy-start(bf16[256,8,128]{0,2,1:T(8,128)(2,1)S(1)} %copy.211) | copy-start | bytes 1572868
  213.7 3.6 copy-start.27
  222.8 3.1 copy-start.18
  223.1 4.3 copy-start.24
  225.9 2.9 copy-start.12
  401.0 2.7 copy-start.13
  401.1 2.7 copy-start.22
  407.2 3.3 copy-start.17
  407.2 9.1 %copy-start.15 = (bf16[256,8,128]{2,0,1:T(8,128)(2,1)}, bf16[256,8,128]{2,0,1:T(8,128)(2,1)S(1)}, u32[]{:S(2)}) copy-start(bf16[256,8,128]{2,0,1:T(8,128)(2,1)S(1)} %get-tuple-element.302) | copy-start | bytes 1572868
  410.9 3.8 copy-start.32
  418.2 2.6 copy-start.23
  430.0 149.8 %all-to-all-start.5 = ((bf16[4,128,1024]{2,1,0:T(8,128)(2,1)}), bf16[4,128,1024]{2,1,0:T(8,128)(2,1)}, u32[]{:S(2)}, u32[]{:S(2)}) async-start(bf16[4,128,1024]{2,1,0:T(8,128)(2,1)} %fusion.7), calls=%async_computation.5 | async-start | bytes 2097152 | tf_op jit(solution)/shard_map/all_to_all | solution.py:207
  568.3 3.0 copy-start.25
  568.3 3.0 copy-start.26
  571.4 4.0 copy-start.1
  575.3 2.5 copy-start.7
  575.3 2.5 copy-start.16
  579.8 166.1 %all-to-all-start.3 = ((bf16[4,128,1024]{2,1,0:T(8,128)(2,1)}), bf16[4,128,1024]{2,1,0:T(8,128)(2,1)}, u32[]{:S(2)}, u32[]{:S(2)}) async-start(bf16[4,128,1024]{2,1,0:T(8,128)(2,1)} %all_to_all.105), calls=%async_computation.3 | async-start | bytes 2097152 | tf_op jit(solution)/shard_map/all_to_all | solution.py:140
  743.5 7.3 copy-start.5
  745.9 6.6 copy-start.14
  745.9 15.4 %all-to-all-start.7 = ((bf16[4,128,1024]{1,2,0:T(8,128)(2,1)}), bf16[4,128,1024]{1,2,0:T(8,128)(2,1)}, u32[]{:S(2)}, u32[]{:S(2)}) async-start(bf16[4,128,1024]{1,2,0:T(8,128)(2,1)} %copy.221), calls=%async_computation.7 | async-start | bytes 2097152 | tf_op jit(solution)/shard_map/all_to_all | solution.py:209
  761.2 14.4 %all-to-all-start.6 = ((bf16[4,128,1024]{1,2,0:T(8,128)(2,1)}), bf16[4,128,1024]{1,2,0:T(8,128)(2,1)S(1)}, u32[]{:S(2)}, u32[]{:S(2)}) async-start(bf16[4,128,1024]{1,2,0:T(8,128)(2,1)} %copy.216), calls=%async_computation.6 | async-start | bytes 2097152 | tf_op jit(solution)/shard_map/all_to_all | solution.py:208
  (13 other events, 21.2 us)
Sparse Core Ops, SparseCore 0:
  48.9 145.0 all-gather.4
  408.5 95.4 all-gather.6
where the time goes:
time: 791 us; the launch traced here: 784 us
  blocking collectives  260 us (33%)
  other arithmetic  191 us (24%)
  local copies, waits for them, and re-layouts  139 us (18%)
  loops' own time  80.8 us (10%)
  starting transfers between devices  41.4 us (5%)
  matrix products  26.3 us (3%)
  waiting for transfers between devices  26 us (3%)
  between operations  19.7 us (2%)
    unnamed x2, blocking collectives  260 us
    select_n x63, other arithmetic, lap(): jnp.where(position < mine, new, old)  93.2 us
    add x63, other arithmetic, linked(): later[0] + (1.0 - later[1]) * earlier[0]  73.2 us
    another operation x1, loops' own time, prefix_2(): return lax.fori_loop(0, ahead, one, state)  43 us
    another operation x1, loops' own time, prefix(): return lax.fori_loop(0, count - 1, lap, so_far)  37.8 us
    dynamic_slice x63, local copies, waits for them, and re-layouts, lap(): longer = join(so_far, jax.tree.map(lambda part: part[position], pieces))  37.2 us
    dynamic_slice x63, local copies, waits for them, and re-layouts, one(): lax.dynamic_index_in_dim(a, source, 0, False).astype(own.dtype)  37.2 us
    unnamed x88, local copies, waits for them, and re-layouts  23.2 us
  transfers between devices with their start and end apart: 10, of which 4 were waited for; matrix products, arithmetic and copies ran while one was open for 26% of the time, Pallas kernels for 0%

commit v1 on v0

--- a/solution.py
+++ b/solution.py
@@ -4,6 +4,15 @@
 from jax.sharding import PartitionSpec as P
 
 DH = 128
+
+
+def part_sources_all_over_axis(target, ax_name):
+    return jnp.concatenate(
+        lax.all_to_all(
+            jnp.stack(jnp.split(target, lax.psum(1, ax_name), axis=1), 0), ax_name, 0, 0
+        ),
+        0,
+    )
 
 
 def prefix(value, axis, join, neutral):
@@ -64,7 +73,7 @@
 def local(queries, keys, values, out_grad, doc_lengths):
     shared = (
         lax.all_to_all(queries, "head", split_axis=1, concat_axis=0, tiled=True),
-        lax.all_to_all(keys, "head", split_axis=1, concat_axis=0, tiled=True),
+        part_sources_all_over_axis(keys, "head"),
         lax.all_to_all(values, "head", split_axis=1, concat_axis=0, tiled=True),
         lax.all_to_all(out_grad, "head", split_axis=1, concat_axis=0, tiled=True),
     )

time: 791 us -> 813 us (1.028)
  waiting for transfers between devices: 26 us -> 35.8 us
  local copies, waits for them, and re-layouts: 139 us -> 148 us
    all_to_all x1, waiting for transfers between devices: 0.01 us -> 8.39 us  [local(): lax.all_to_all(queries, 'head', split_axis=1, concat_axis=0, tiled=True)]
    unnamed x88 -> x94, local copies, waits for them, and re-layouts: 23.2 us -> 24.4 us
  transfers between devices with their start and end apart: 10 -> 10, of which waited for: 4 -> 5; matrix products, arithmetic and copies ran while one was open for 26% -> 26% of each run, Pallas kernels for 0% -> 0%
where the time goes in v1:
time: 813 us; the launch traced here: 806 us
  blocking collectives  260 us (32%)
  other arithmetic  191 us (23%)
  local copies, waits for them, and re-layouts  148 us (18%)
  loops' own time  84.5 us (10%)
  starting transfers between devices  40.7 us (5%)
  waiting for transfers between devices  35.8 us (4%)
  matrix products  26.2 us (3%)
  between operations  19.7 us (2%)
    unnamed x2, blocking collectives  260 us
    select_n x63, other arithmetic, lap(): jnp.where(position < mine, new, old)  93.1 us
    add x63, other arithmetic, linked(): later[0] + (1.0 - later[1]) * earlier[0]  73.2 us
    another operation x1, loops' own time, prefix_2(): return lax.fori_loop(0, ahead, one, state)  43 us
    another operation x1, loops' own time, prefix(): return lax.fori_loop(0, count - 1, lap, so_far)  41.5 us
    dynamic_slice x63, local copies, waits for them, and re-layouts, lap(): longer = join(so_far, jax.tree.map(lambda part: part[position], pieces))  40.9 us
    dynamic_slice x63, local copies, waits for them, and re-layouts, one(): lax.dynamic_index_in_dim(a, source, 0, False).astype(own.dtype)  37.2 us
    unnamed x94, local copies, waits for them, and re-layouts  24.4 us
  transfers between devices with their start and end apart: 10, of which 5 were waited for; matrix products, arithmetic and copies ran while one was open for 26% of the time, Pallas kernels for 0%

profile of v1, /device:TPU:8, one launch (start us, length us, event | category | flops | bytes accessed | tf_op | source)
XLA Modules:
  0.0 805.5 jit_solution(13202837127730200551)
XLA Ops:
  9.5 5.6 all-to-all-start.1
  16.3 11.8 %all-to-all-done.1 = bf16[4,128,1024]{2,1,0:T(8,128)(2,1)S(1)} async-done(((bf16[4,128,1024]{2,1,0:T(8,128)(2,1)}), bf16[4,128,1024]{2,1,0:T(8,128)(2,1)S(1)}, u32[]{:S(2)}, u32[]{:S(2)}) %all-to-all-start.1) | async-done | bytes 1048608 | tf_op jit(solution)/shard_map/all_to_all | solution.py:11
  28.1 4.9 all-to-all-start.2
  37.5 7.6 all-to-all-done.2
  49.9 4.9 all-to-all-start
  57.4 8.4 %all-to-all-done = bf16[128,4,1024]{0,2,1:T(8,128)(2,1)S(1)} async-done(((bf16[128,4,1024]{0,2,1:T(8,128)(2,1)}), bf16[128,4,1024]{0,2,1:T(8,128)(2,1)S(1)}, u32[]{:S(2)}, u32[]{:S(2)}) %all-to-all-start) | async-done | bytes 1048608 | tf_op jit(solution)/shard_map/all_to_all | solution.py:75
  65.8 5.7 all-to-all-start.4
  76.8 134.0 %all-reduce.2 = f32[64]{0:T(128)S(1)} all-reduce(f32[64]{0:T(128)S(1)} %dynamic-update-slice.10), channel_id=1, replica_groups=mesh['seq'=64,'head'=4] {'seq'}, use_global_device_ids=true, to_apply=%add.2 | all-reduce | flops 64 | bytes 512
  213.1 2.7 fusion.23
  225.1 2.5 slice_convert_fusion.1
  232.3 2.5 copy.303
  235.0 2.6 bitcast_select_fusion
  244.5 175.6 %while.35 = (s32[]{:T(128)}, f32[8,128,128]{2,1,0:T(8,128)S(1)}, s32[]{:T(128)}, f32[64,8,128,128]{3,2,1,0:T(8,128)}, f32[64]{0:T(128)S(1)}, /*index=5*/s32[]{:T(128)}, f32[1]{0:T(128)}, s32[]{:T(128)}) while((s32[]{:T(128)}, f32[8,128,128]{2,1,0:T(8,128)S(1)}, s32[]{:T(128)}, f32[64,8,128,128]{3,2,1,0:T(8,128)}, f32[64]{0:T(128)S(1)}, ...), condition=%wide.region_4.5_spmd.clone, body=%wide.region_3.4_spmd.clone.sunk | while | flops 524293 | bytes 1573001 | solution.py:29
  431.3 2.5 copy.254
  437.3 2.6 copy.261
  439.9 2.9 pad_maximum_fusion
  442.8 2.9 copy.262
  445.7 3.0 copy.263
  448.7 3.1 fusion.7
  451.8 4.8 all-to-all-start.5
  460.0 125.6 %all-reduce.3 = bf16[64]{0:T(256)(128)(2,1)S(1)} all-reduce(bf16[64]{0:T(256)(128)(2,1)S(1)} %dynamic-update-slice.11), channel_id=1, replica_groups=mesh['seq'=64,'head'=4] {'seq'}, use_global_device_ids=true, to_apply=%add.3 | all-reduce | flops 64 | bytes 256
  585.6 3.4 copy.305
  589.1 3.0 copy.291
  596.1 2.5 convolution_bitcast_fusion.1
  600.5 4.8 all-to-all-start.3
  605.3 153.4 %while.34 = (s32[]{:T(128)}, f32[8,128,128]{2,1,0:T(8,128)S(1)}, s32[]{:T(128)}, bf16[64,8,128,128]{3,2,1,0:T(8,128)(2,1)}, bf16[64]{0:T(256)(128)(2,1)S(1)}, /*...) while((s32[]{:T(128)}, f32[8,128,128]{2,1,0:T(8,128)S(1)}, s32[]{:T(128)}, ...), condition=%wide.region_11.12_spmd, body=%wide.region_10.11_spmd.sunk | while | flops 393223 | bytes 1310893 | solution.py:52
  758.7 3.4 fusion.12
  764.2 2.4 copy.275
  766.6 4.9 all-to-all-start.7
  777.1 5.5 all-to-all-done.7
  782.6 4.9 all-to-all-start.6
  795.0 2.4 all-to-all-done.6
  (413 shorter events, 323.1 us)
Async XLA Ops:
  8.4 6.8 copy-start.32
  9.5 18.5 %all-to-all-start.1 = ((bf16[4,128,1024]{2,1,0:T(8,128)(2,1)}), bf16[4,128,1024]{2,1,0:T(8,128)(2,1)S(1)}, u32[]{:S(2)}, u32[]{:S(2)}) async-start(bf16[4,128,1024]{2,1,0:T(8,128)(2,1)} %pad_maximum_fusion.1), calls=%async_computation.1 | async-start | bytes 2097152 | tf_op jit(solution)/shard_map/all_to_all | solution.py:11
  15.2 17.9 %copy-start.36 = (s32[8]{0:T(128)S(1)}, s32[8]{0:T(128)}, u32[]{:S(2)}) copy-start(s32[8]{0:T(128)} %param.25) | copy-start | bytes 100
  28.1 17.0 %all-to-all-start.2 = ((bf16[128,4,1024]{2,0,1:T(8,128)(2,1)}), bf16[128,4,1024]{2,0,1:T(8,128)(2,1)S(1)}, u32[]{:S(2)}, u32[]{:S(2)}) async-start(bf16[128,4,1024]{2,0,1:T(8,128)(2,1)} %bitcast.158), calls=%async_computation.2 | async-start | bytes 2097152 | tf_op jit(solution)/shard_map/all_to_all | solution.py:77
  33.0 211.5 %all-gather.5.cloned.1.call-start = ((), (), s32[]{:S(2)}) async-start(), calls=%async_computation.8 | async-start | bytes 34078720 | tf_op jit(solution)/shard_map/all_gather | solution.py:20
  37.2 7.9 copy-start.14
  49.9 15.8 %all-to-all-start = ((bf16[128,4,1024]{0,2,1:T(8,128)(2,1)}), bf16[128,4,1024]{0,2,1:T(8,128)(2,1)S(1)}, u32[]{:S(2)}, u32[]{:S(2)}) async-start(bf16[128,4,1024]{0,2,1:T(8,128)(2,1)} %bitcast.189), calls=%async_computation | async-start | bytes 2097152 | tf_op jit(solution)/shard_map/all_to_all | solution.py:75
  54.9 20.6 %copy-start.37 = (u32[256]{0:T(256)S(1)}, u32[256]{0:T(256)}, u32[]{:S(2)}) copy-start(u32[256]{0:T(256)} %constant.223) | copy-start | bytes 3076
  65.8 6.4 copy-start.2
  65.8 159.3 %all-to-all-start.4 = ((bf16[128,4,1024]{2,0,1:T(8,128)(2,1)}), bf16[128,4,1024]{2,0,1:T(8,128)(2,1)}, u32[]{:S(2)}, u32[]{:S(2)}) async-start(bf16[128,4,1024]{2,0,1:T(8,128)(2,1)} %bitcast.186), calls=%async_computation.4 | async-start | bytes 2097152 | tf_op jit(solution)/shard_map/all_to_all | solution.py:78
  71.5 533.9 %all-gather.7.cloned.1.call-start = ((), (), s32[]{:S(2)}) async-start(), calls=%async_computation.9 | async-start | bytes 17039360 | tf_op jit(solution)/shard_map/all_gather | solution.py:37
  222.9 197.3 %copy-start.6 = (bf16[256,8,128]{0,2,1:T(8,128)(2,1)}, bf16[256,8,128]{0,2,1:T(8,128)(2,1)S(1)}, u32[]{:S(2)}) copy-start(bf16[256,8,128]{0,2,1:T(8,128)(2,1)S(1)} %reshape.298) | copy-start | bytes 1572868
  225.1 3.6 copy-start.30
  234.8 2.9 copy-start.21
  235.0 4.1 copy-start.27
  237.7 2.9 copy-start.15
  237.7 2.9 copy-start.34
  420.2 2.7 copy-start.16
  420.2 2.7 copy-start.24
  426.3 3.2 copy-start.20
  426.3 9.1 %copy-start.18 = (bf16[256,8,128]{2,0,1:T(8,128)(2,1)}, bf16[256,8,128]{2,0,1:T(8,128)(2,1)S(1)}, u32[]{:S(2)}) copy-start(bf16[256,8,128]{2,0,1:T(8,128)(2,1)S(1)} %get-tuple-element.306) | copy-start | bytes 1572868
  430.0 3.8 copy-start.35
  445.7 3.0 copy-start.3
  451.8 148.7 %all-to-all-start.5 = ((bf16[4,128,1024]{1,2,0:T(8,128)(2,1)}), bf16[4,128,1024]{1,2,0:T(8,128)(2,1)}, u32[]{:S(2)}, u32[]{:S(2)}) async-start(bf16[4,128,1024]{1,2,0:T(8,128)(2,1)} %fusion.7), calls=%async_computation.5 | async-start | bytes 2097152 | tf_op jit(solution)/shard_map/all_to_all | solution.py:216
  589.1 3.0 copy-start.28
  589.1 3.0 copy-start.29
  592.1 4.0 copy-start.1
  600.5 166.1 %all-to-all-start.3 = ((bf16[4,128,1024]{2,1,0:T(8,128)(2,1)}), bf16[4,128,1024]{2,1,0:T(8,128)(2,1)}, u32[]{:S(2)}, u32[]{:S(2)}) async-start(bf16[4,128,1024]{2,1,0:T(8,128)(2,1)} %all_to_all.97), calls=%async_computation.3 | async-start | bytes 2097152 | tf_op jit(solution)/shard_map/all_to_all | solution.py:149
  764.2 7.3 copy-start.7
  766.6 6.6 copy-start.17
  766.6 16.0 %all-to-all-start.7 = ((bf16[4,128,1024]{1,2,0:T(8,128)(2,1)}), bf16[4,128,1024]{1,2,0:T(8,128)(2,1)}, u32[]{:S(2)}, u32[]{:S(2)}) async-start(bf16[4,128,1024]{1,2,0:T(8,128)(2,1)} %copy.275), calls=%async_computation.7 | async-start | bytes 2097152 | tf_op jit(solution)/shard_map/all_to_all | solution.py:218
  782.6 14.8 %all-to-all-start.6 = ((bf16[4,128,1024]{1,2,0:T(8,128)(2,1)}), bf16[4,128,1024]{1,2,0:T(8,128)(2,1)S(1)}, u32[]{:S(2)}, u32[]{:S(2)}) async-start(bf16[4,128,1024]{1,2,0:T(8,128)(2,1)} %copy.270), calls=%async_computation.6 | async-start | bytes 2097152 | tf_op jit(solution)/shard_map/all_to_all | solution.py:217
  (16 other events, 28.9 us)
Sparse Core Ops, SparseCore 0:
  48.7 145.0 all-gather.4
  427.6 95.6 all-gather.6
